TPU v7x, 32 devices: a whole 2x2x4 slice. The times are simulated.
32 devices in a mesh: scene: 4 (over y, x), row: 4 (over z), col: 2 (over core).
Axes of the slice: x: 2, y: 2, z: 4, core: 2. Of those that a mesh axis runs over, the one named last changes fastest.
Arguments:
- scenes: bfloat16 [4, 256, 128, 128], P('scene', 'row', 'col'), may hold values from -6 to 6
- cotangent: bfloat16 [4, 256, 128, 128], P('scene', 'row', 'col'), may hold values from -0.016479492 to 0.016479492
- params: float32 [294912], P(('scene', 'row', 'col')), may hold values from -0.1875 to 0.1875
- partials: float32 [32, 294912], P(('scene', 'row', 'col')), may hold values from -8 to 8
Outputs:
- sam_grad: float32 [294912], P(('scene', 'row', 'col'))
All inputs are finite; a program needn't handle non-finite values.
Results may differ from a plain program's by a relative error of at most 0.0042.
Values may be sent and summed in bfloat16 or wider, within the bound.
A program may use at most 64 MiB of HBM per device.

v0:
```python
import jax
import jax.numpy as jnp
from jax import lax
from jax.sharding import PartitionSpec as P

radius = 2.0
epsilon = 1e-06


def with_halo(cells, sides, width):
    for axis, dim in sides:
        count = lax.axis_size(axis)
        ends = count - 1
        head = lax.slice_in_dim(cells, 0, width, axis=dim)
        tail = lax.slice_in_dim(cells, cells.shape[dim] - width, cells.shape[dim], axis=dim)
        cells = jnp.concatenate(
            [
                lax.ppermute(tail, axis, [(i, (i + 1) % count) for i in range(ends)]),
                cells,
                lax.ppermute(head, axis, [((i + 1) % count, i) for i in range(ends)]),
            ],
            axis=dim,
        )
    return cells


def convolve(padded, kernel):
    return lax.conv_general_dilated(
        padded,
        kernel,
        (1, 1),
        "VALID",
        dimension_numbers=("NHWC", "HWIO", "NHWC"),
        preferred_element_type=jnp.float32,
    )


def widened(field):
    return with_halo(field, (("row", 1), ("col", 2)), 1)


def kernel_grad(padded, errors):
    height = errors.shape[1]
    width = errors.shape[2]
    rows_out = []
    for row_off in range(3):
        cols_out = []
        for col_off in range(3):
            window = padded[:, row_off : row_off + height, col_off : col_off + width, :]
            cols_out.append(
                jnp.einsum("nhwc,nhwd->cd", window, errors, preferred_element_type=jnp.float32)
            )
        rows_out.append(jnp.stack(cols_out))
    return jnp.stack(rows_out)


def on_device(scenes, cotangent, params, partials):
    local_part = partials[0]
    totals = lax.psum(local_part, ("scene", "row", "col"))
    raw_whole = lax.all_gather(params, ("scene", "row", "col"), axis=0, tiled=True)
    factor = radius / (jnp.sqrt(jnp.sum(totals * totals)) + epsilon)
    whole = (raw_whole + factor * totals).astype(jnp.bfloat16)
    channels = scenes.shape[3]
    kernels = whole.reshape(2, 3, 3, channels, channels)
    kernel_one = kernels[0]
    flipped = jnp.transpose(kernels[1][::-1, ::-1], (0, 1, 3, 2))
    padded_in = widened(scenes)
    pre = convolve(padded_in, kernel_one)
    hidden = jax.nn.silu(pre).astype(jnp.bfloat16)
    back = convolve(widened(cotangent), flipped)
    squash = jax.nn.sigmoid(pre)
    delta = (back * squash * (1.0 + pre * (1.0 - squash))).astype(jnp.bfloat16)
    grad_one = kernel_grad(padded_in, delta)
    grad_two = kernel_grad(widened(hidden), cotangent)
    local_grad = jnp.stack([grad_one, grad_two]).reshape(-1)
    return lax.psum_scatter(local_grad, ("scene", "row", "col"), scatter_dimension=0, tiled=True)


def solution(mesh):
    return jax.shard_map(
        on_device,
        mesh=mesh,
        in_specs=(
            P("scene", "row", "col", None),
            P("scene", "row", "col", None),
            P(("scene", "row", "col")),
            P(("scene", "row", "col"), None),
        ),
        out_specs=P(("scene", "row", "col")),
        check_vma=False,
    )
```

profile of v0, /device:TPU:0, one launch (start us, length us, event | category | flops | bytes accessed | tf_op | source)
XLA Modules:
  0.0 384.6 jit_solution(3427847306633833855)
XLA Ops:
  8.1 5.1 %collective-permute-start = (bf16[1,1,64,128]{3,2,1,0:T(8,128)(2,1)S(1)}, bf16[1,1,64,128]{3,2,1,0:T(8,128)(2,1)S(1)}, u32[]{:S(2)}, u32[]{:S(2)}) collective-permute-start(bf16[1,1,64,128]{3,2,1,0:T(8,128)(2,1)S(1)} %get-tuple-element.18), channel_id=1, source_target_pairs={{0,2},{2,4},{4,6},{1,3},{3,5},{5,7},{8,10},{10,12},{12,14},{9,11},... | collective-permute-start | bytes 49160 | tf_op jit(solution)/shard_map/ppermute | solution.py:18
  15.2 4.5 %collective-permute-start.3 = (bf16[1,1,64,128]{3,2,1,0:T(8,128)(2,1)S(1)}, bf16[1,1,64,128]{3,2,1,0:T(8,128)(2,1)S(1)}, u32[]{:S(2)}, u32[]{:S(2)}) collective-permute-start(bf16[1,1,64,128]{3,2,1,0:T(8,128)(2,1)S(1)} %get-tuple-element.16), channel_id=1, source_target_pairs={{0,2},{2,4},{4,6},{1,3},{3,5},{5,7},{8,10},{10,12},{12,14},{9,11},... | collective-permute-start | bytes 49160 | tf_op jit(solution)/shard_map/ppermute | solution.py:18
  25.5 2.9 collective-permute-start.5
  34.5 112.6 %all-reduce.4.cloned.1.call-done = f32[294912]{0:T(1024)} async-done(((f32[294912]{0:T(1024)}), f32[294912]{0:T(1024)}) %all-reduce.4.cloned.1.call-update) | async-done | bytes 1179664 | tf_op jit(solution)/shard_map/psum | solution.py:59
  147.1 2.3 multiply_reduce_fusion
  150.2 53.1 %all-gather.2.cloned.1.call-done = f32[294912]{0:T(1024)} async-done(((f32[9216]{0:T(1024)}), f32[294912]{0:T(1024)}) %all-gather.2.cloned.1.call-update) | async-done | bytes 1179664 | tf_op jit(solution)/shard_map/all_gather | solution.py:60
  203.2 1.5 add_convert_fusion
  204.8 3.2 multiply_convert_fusion.1
  209.4 3.4 multiply_convert_fusion
  214.4 1.3 convolution_bitcast_fusion.13
  215.8 2.5 collective-permute-start.8
  218.4 1.6 collective-permute-start.9
  220.0 2.1 convolution_bitcast_fusion.4
  222.1 1.4 convolution_bitcast_fusion.11
  223.5 1.4 convolution_bitcast_fusion.9
  224.9 1.3 convolution_bitcast_fusion.10
  226.2 1.4 convolution_bitcast_fusion.14
  227.6 1.4 convolution_bitcast_fusion.12
  229.0 1.4 convolution_bitcast_fusion.17
  230.4 1.4 convolution_bitcast_fusion.15
  231.8 1.3 convolution_bitcast_fusion.16
  234.3 1.8 collective-permute-start.10
  244.2 132.5 %all-reduce.6.cloned.1.call-done = f32[294912]{0:T(1024)} async-done(((f32[294912]{0:T(1024)}), f32[294912]{0:T(1024)}) %all-reduce.6.cloned.1.call-update) | async-done | bytes 1179664
  376.7 1.4 dynamic-slice
  (106 shorter events, 27.2 us)
Async XLA Ops:
  6.5 1.5 copy-start.3
  6.5 140.6 %all-reduce.4.cloned.1.call-start = ((), (), s32[]{:S(2)}) async-start(), calls=%async_computation.1 | async-start | bytes 2359296 | tf_op jit(solution)/shard_map/psum | solution.py:59
  7.3 196.0 %all-gather.2.cloned.1.call-start = ((), (), s32[]{:S(2)}) async-start(), calls=%async_computation | async-start | bytes 1216512 | tf_op jit(solution)/shard_map/all_gather | solution.py:60
  8.0 368.7 %all-reduce.6.cloned.1.call-start = ((), (), s32[]{:S(2)}) async-start(), calls=%async_computation.2 | async-start | bytes 2359296
  8.1 17.1 %copy-start.5 = (bf16[1,64,64,128]{3,2,1,0:T(8,128)(2,1)S(1)}, bf16[1,64,64,128]{3,2,1,0:T(8,128)(2,1)}, u32[]{:S(2)}) copy-start(bf16[1,64,64,128]{3,2,1,0:T(8,128)(2,1)} %param.5) | copy-start | bytes 3145732
  8.1 13.0 %collective-permute-start = (bf16[1,1,64,128]{3,2,1,0:T(8,128)(2,1)S(1)}, bf16[1,1,64,128]{3,2,1,0:T(8,128)(2,1)S(1)}, u32[]{:S(2)}, u32[]{:S(2)}) collective-permute-start(bf16[1,1,64,128]{3,2,1,0:T(8,128)(2,1)S(1)} %get-tuple-element.18), channel_id=1, source_target_pairs={{0,2},{2,4},{4,6},{1,3},{3,5},{5,7},{8,10},{10,12},{12,14},{9,11},... | collective-permute-start | bytes 49160 | tf_op jit(solution)/shard_map/ppermute | solution.py:18
  13.2 8.6 %collective-permute-start.1 = (bf16[1,1,64,128]{3,2,1,0:T(8,128)(2,1)S(1)}, bf16[1,1,64,128]{3,2,1,0:T(8,128)(2,1)S(1)}, u32[]{:S(2)}, u32[]{:S(2)}) collective-permute-start(bf16[1,1,64,128]{3,2,1,0:T(8,128)(2,1)S(1)} %get-tuple-element.17), channel_id=1, source_target_pairs={{2,0},{4,2},{6,4},{3,1},{5,3},{7,5},{10,8},{12,10},{14,12},{11,9},... | collective-permute-start | bytes 49160 | tf_op jit(solution)/shard_map/ppermute | solution.py:20
  15.2 9.9 %collective-permute-start.3 = (bf16[1,1,64,128]{3,2,1,0:T(8,128)(2,1)S(1)}, bf16[1,1,64,128]{3,2,1,0:T(8,128)(2,1)S(1)}, u32[]{:S(2)}, u32[]{:S(2)}) collective-permute-start(bf16[1,1,64,128]{3,2,1,0:T(8,128)(2,1)S(1)} %get-tuple-element.16), channel_id=1, source_target_pairs={{0,2},{2,4},{4,6},{1,3},{3,5},{5,7},{8,10},{10,12},{12,14},{9,11},... | collective-permute-start | bytes 49160 | tf_op jit(solution)/shard_map/ppermute | solution.py:18
  19.8 5.6 %collective-permute-start.4 = (bf16[1,1,64,128]{3,2,1,0:T(8,128)(2,1)S(1)}, bf16[1,1,64,128]{3,2,1,0:T(8,128)(2,1)S(1)}, u32[]{:S(2)}, u32[]{:S(2)}) collective-permute-start(bf16[1,1,64,128]{3,2,1,0:T(8,128)(2,1)S(1)} %get-tuple-element.15), channel_id=1, source_target_pairs={{2,0},{4,2},{6,4},{3,1},{5,3},{7,5},{10,8},{12,10},{14,12},{11,9},... | collective-permute-start | bytes 49160 | tf_op jit(solution)/shard_map/ppermute | solution.py:20
  22.5 7.2 %collective-permute-start.2 = (bf16[1,66,1,128]{3,2,1,0:T(2,128)(2,1)S(1)}, bf16[1,66,1,128]{3,2,1,0:T(2,128)(2,1)S(1)}, u32[]{:S(2)}, u32[]{:S(2)}) collective-permute-start(bf16[1,66,1,128]{3,2,1,0:T(2,128)(2,1)S(1)} %get-tuple-element.13), channel_id=1, source_target_pairs={{0,1},{2,3},{4,5},{6,7},{8,9},{10,11},{12,13},{14,15},{16,17},{18,... | collective-permute-start | bytes 50696 | tf_op jit(solution)/shard_map/ppermute | solution.py:18
  23.8 5.9 %collective-permute-start.7 = (bf16[1,66,1,128]{3,2,1,0:T(2,128)(2,1)S(1)}, bf16[1,66,1,128]{3,2,1,0:T(2,128)(2,1)S(1)}, u32[]{:S(2)}, u32[]{:S(2)}) collective-permute-start(bf16[1,66,1,128]{3,2,1,0:T(2,128)(2,1)S(1)} %get-tuple-element.14), channel_id=1, source_target_pairs={{1,0},{3,2},{5,4},{7,6},{9,8},{11,10},{13,12},{15,14},{17,16},{19,... | collective-permute-start | bytes 50696 | tf_op jit(solution)/shard_map/ppermute | solution.py:20
  25.5 6.1 %collective-permute-start.5 = (bf16[1,66,1,128]{3,2,1,0:T(2,128)(2,1)S(1)}, bf16[1,66,1,128]{3,2,1,0:T(2,128)(2,1)S(1)}, u32[]{:S(2)}, u32[]{:S(2)}) collective-permute-start(bf16[1,66,1,128]{3,2,1,0:T(2,128)(2,1)S(1)} %get-tuple-element.7), channel_id=1, source_target_pairs={{0,1},{2,3},{4,5},{6,7},{8,9},{10,11},{12,13},{14,15},{16,17},{18,... | collective-permute-start | bytes 50696 | tf_op jit(solution)/shard_map/ppermute | solution.py:18
  28.4 3.2 collective-permute-start.6
  147.1 56.1 %copy-start = (f32[294912]{0:T(1024)S(1)}, f32[294912]{0:T(1024)}, u32[]{:S(2)}) copy-start(f32[294912]{0:T(1024)} %all-reduce.4.cloned.1.call-done) | copy-start | bytes 3538948
  150.1 54.7 %copy-start.15 = (pred[8,9]{0,1:T(8,128)(4,1)S(1)}, pred[8,9]{0,1:T(8,128)(4,1)}, u32[]{:S(2)}) copy-start(pred[8,9]{0,1:T(8,128)(4,1)} %constant.21) | copy-start | bytes 220
  203.2 1.6 copy-start.9
  215.8 18.3 %collective-permute-start.8 = (bf16[1,1,64,128]{3,2,1,0:T(8,128)(2,1)S(1)}, bf16[1,1,64,128]{3,2,1,0:T(8,128)(2,1)S(1)}, u32[]{:S(2)}, u32[]{:S(2)}) collective-permute-start(bf16[1,1,64,128]{3,2,1,0:T(8,128)(2,1)S(1)} %slice.186), channel_id=1, source_target_pairs={{0,2},{2,4},{4,6},{1,3},{3,5},{5,7},{8,10},{10,12},{12,14},{9,11},... | collective-permute-start | bytes 49160 | tf_op jit(solution)/shard_map/ppermute | solution.py:18
  218.3 3.7 copy-start.8
  218.4 15.8 %collective-permute-start.9 = (bf16[1,1,64,128]{3,2,1,0:T(8,128)(2,1)S(1)}, bf16[1,1,64,128]{3,2,1,0:T(8,128)(2,1)S(1)}, u32[]{:S(2)}, u32[]{:S(2)}) collective-permute-start(bf16[1,1,64,128]{3,2,1,0:T(8,128)(2,1)S(1)} %slice.189), channel_id=1, source_target_pairs={{2,0},{4,2},{6,4},{3,1},{5,3},{7,5},{10,8},{12,10},{14,12},{11,9},... | collective-permute-start | bytes 49160 | tf_op jit(solution)/shard_map/ppermute | solution.py:20
  223.5 1.4 copy-start.14
  230.4 1.4 copy-start.12
  233.2 4.2 %copy-start.6 = (bf16[1,64,64,128]{3,2,1,0:T(8,128)(2,1)S(1)}, bf16[1,64,64,128]{3,2,1,0:T(8,128)(2,1)}, u32[]{:S(2)}) copy-start(bf16[1,64,64,128]{3,2,1,0:T(8,128)(2,1)} %param.5) | copy-start | bytes 3145732
  234.3 4.1 %collective-permute-start.10 = (bf16[1,66,1,128]{3,2,1,0:T(2,128)(2,1)S(1)}, bf16[1,66,1,128]{3,2,1,0:T(2,128)(2,1)S(1)}, u32[]{:S(2)}, u32[]{:S(2)}) collective-permute-start(bf16[1,66,1,128]{3,2,1,0:T(2,128)(2,1)S(1)} %get-tuple-element.11), channel_id=1, source_target_pairs={{0,1},{2,3},{4,5},{6,7},{8,9},{10,11},{12,13},{14,15},{16,17},{18,... | collective-permute-start | bytes 50696 | tf_op jit(solution)/shard_map/ppermute | solution.py:18
  236.1 3.1 collective-permute-start.11
  (7 other events, 7.4 us)
Sparse Core Ops, SparseCore 0:
  12.7 134.3 all-reduce.3
  150.1 53.0 all-gather.1
  244.3 132.3 all-reduce.5
where the time goes:
time: 385 us
  waiting for transfers between devices  301 us (78%)
  starting transfers between devices  26.3 us (7%)
  matrix products  24.9 us (6%)
  between operations  14.5 us (4%)
  local copies, waits for them, and re-layouts  11.1 us (3%)
  other arithmetic  7.21 us (2%)
    unnamed x4, waiting for transfers between devices  134 us
    psum x1, waiting for transfers between devices, on_device(): totals = lax.psum(local_part, ('scene', 'row', 'col'))  113 us
    all_gather x1, waiting for transfers between devices, on_device(): lax.all_gather(params, ('scene', 'row', 'col'), axis=0, tiled=True)  53.1 us
    dot_general x18, matrix products, kernel_grad(): jnp.einsum('nhwc,nhwd->cd', window, errors, preferred_element_type=jnp.fl...  18.2 us
    ppermute x6, starting transfers between devices, with_halo(): lax.ppermute(tail, axis, [(i, (i + 1) % count) for i in range(ends)])  18.1 us
    ppermute x6, starting transfers between devices, with_halo(): lax.ppermute(head, axis, [((i + 1) % count, i) for i in range(ends)])  8.06 us
  transfers between devices with their start and end apart: 15, of which 5 were waited for; matrix products, arithmetic and copies ran while one was open for 6% of the time, Pallas kernels for 0%

commit v1 on v0

--- a/solution.py
+++ b/solution.py
@@ -56,7 +56,7 @@
 
 def on_device(scenes, cotangent, params, partials):
     local_part = partials[0]
-    totals = lax.psum(local_part, ("scene", "row", "col"))
+    totals = lax.psum(lax.psum(local_part, "scene"), ("row", "col"))
     raw_whole = lax.all_gather(params, ("scene", "row", "col"), axis=0, tiled=True)
     factor = radius / (jnp.sqrt(jnp.sum(totals * totals)) + epsilon)
     whole = (raw_whole + factor * totals).astype(jnp.bfloat16)

time: 385 us -> 317 us (0.82)
  waiting for transfers between devices: 301 us -> 234 us
    all_gather x1, waiting for transfers between devices: 53.1 us -> 0.03 us  [on_device(): lax.all_gather(params, ('scene', 'row', 'col'), axis=0, tiled=True)]
    psum x1 -> x2, waiting for transfers between devices: 113 us -> 98.8 us  [on_device(): totals = lax.psum(lax.psum(local_part, 'scene'), ('row', 'col'))]
    unnamed x4 -> x5, waiting for transfers between devices: 134 us -> 133 us
  transfers between devices with their start and end apart: 15 -> 16, of which waited for: 5 -> 5; matrix products, arithmetic and copies ran while one was open for 6% -> 7% of each run, Pallas kernels for 0% -> 0%
where the time goes in v1:
time: 317 us; the launch traced here: 316 us
  waiting for transfers between devices  234 us (74%)
  matrix products  24.9 us (8%)
  starting transfers between devices  24.1 us (8%)
  between operations  16.3 us (5%)
  local copies, waits for them, and re-layouts  9.82 us (3%)
  other arithmetic  7.18 us (2%)
    unnamed x5, waiting for transfers between devices  133 us
    psum x2, waiting for transfers between devices, on_device(): totals = lax.psum(lax.psum(local_part, 'scene'), ('row', 'col'))  98.8 us
    dot_general x18, matrix products, kernel_grad(): jnp.einsum('nhwc,nhwd->cd', window, errors, preferred_element_type=jnp.fl...  18.2 us
    ppermute x6, starting transfers between devices, with_halo(): lax.ppermute(tail, axis, [(i, (i + 1) % count) for i in range(ends)])  16 us
    ppermute x6, starting transfers between devices, with_halo(): lax.ppermute(head, axis, [((i + 1) % count, i) for i in range(ends)])  8.06 us
    unnamed x40, local copies, waits for them, and re-layouts  6.72 us
    conv_general_dilated x2, matrix products, convolve(): lax.conv_general_dilated(padded, kernel, (1, 1), 'VALID', dimension_numbe...  6.66 us
  transfers between devices with their start and end apart: 16, of which 5 were waited for; matrix products, arithmetic and copies ran while one was open for 7% of the time, Pallas kernels for 0%

profile of v1, /device:TPU:0, one launch (start us, length us, event | category | flops | bytes accessed | tf_op | source)
XLA Modules:
  0.0 316.0 jit_solution(9491792473995955053)
XLA Ops:
  8.1 60.2 %all-reduce.5.cloned.1.call-done = f32[294912]{0:T(1024)} async-done(((f32[294912]{0:T(1024)}), f32[294912]{0:T(1024)}) %all-reduce.5.cloned.1.call-update) | async-done | bytes 1179664 | tf_op jit(solution)/shard_map/psum | solution.py:59
  69.0 3.4 %collective-permute-start = (bf16[1,1,64,128]{3,2,1,0:T(8,128)(2,1)S(1)}, bf16[1,1,64,128]{3,2,1,0:T(8,128)(2,1)S(1)}, u32[]{:S(2)}, u32[]{:S(2)}) collective-permute-start(bf16[1,1,64,128]{3,2,1,0:T(8,128)(2,1)S(1)} %get-tuple-element.18), channel_id=1, source_target_pairs={{0,2},{2,4},{4,6},{1,3},{3,5},{5,7},{8,10},{10,12},{12,14},{9,11},... | collective-permute-start | bytes 49160 | tf_op jit(solution)/shard_map/ppermute | solution.py:18
  72.4 1.3 collective-permute-start.1
  73.8 4.5 %collective-permute-start.3 = (bf16[1,1,64,128]{3,2,1,0:T(8,128)(2,1)S(1)}, bf16[1,1,64,128]{3,2,1,0:T(8,128)(2,1)S(1)}, u32[]{:S(2)}, u32[]{:S(2)}) collective-permute-start(bf16[1,1,64,128]{3,2,1,0:T(8,128)(2,1)S(1)} %get-tuple-element.16), channel_id=1, source_target_pairs={{0,2},{2,4},{4,6},{1,3},{3,5},{5,7},{8,10},{10,12},{12,14},{9,11},... | collective-permute-start | bytes 49160 | tf_op jit(solution)/shard_map/ppermute | solution.py:18
  84.1 2.3 collective-permute-start.5
  92.5 38.6 %all-reduce.7.cloned.1.call-done = f32[294912]{0:T(1024)} async-done(((f32[294912]{0:T(1024)}), f32[294912]{0:T(1024)}) %all-reduce.7.cloned.1.call-update) | async-done | bytes 1179664 | tf_op jit(solution)/shard_map/psum | solution.py:59
  131.1 2.3 multiply_reduce_fusion
  134.1 1.5 add_convert_fusion
  135.7 3.2 %multiply_convert_fusion.1 = (bf16[64,8,9,128]{3,1,2,0:T(8,128)(2,1)S(1)}, f32[64,8,9,128]{3,1,2,0:T(8,128)S(1)}) fusion(pred[8,9]{0,1:T(8,128)(4,1)S(1)} %copy-done.15, bf16[3,3,128,128]{3,2,1,0:T(8,128)(2,1)S(1)} %bitcast.193, bf16[66,1,7,2,128]{4,2,3,0,1:T(8,128)(2,1)S(1)} %copy-done.9, bf16[66,1,8,9,128]{4,2,3,0,1:T(8,128)(2,1)S(1)} %copy.24), kind=kOutput, calls=%fused_computation.4 | convolution fusion | flops 1366953984 | bytes 5286984 | tf_op jit(solution)/shard_map/conv_general_dilated | solution.py:28
  140.3 3.4 %multiply_convert_fusion = bf16[64,8,9,128]{3,1,2,0:T(8,128)(2,1)S(1)} fusion(f32[64,8,9,128]{3,1,2,0:T(8,128)S(1)} %get-tuple-element.22, bf16[3,3,128,128]{3,2,1,0:T(8,128)(2,1)S(1)} %bitcast.192, bf16[66,1,7,2,128]{4,2,3,0,1:T(8,128)(2,1)S(1)} %copy-done.10, bf16[66,1,8,9,128]{4,2,3,0,1:T(8,128)(2,1)S(1)} %copy-done.2, pred[8,9]{0,1:T(8,128)(4,1)S(1)} %copy-done.15), kind=kOutput, calls=%fused_computation.3 | convolution fusion | flops 1369903104 | bytes 5286984 | tf_op jit(solution)/shard_map/conv_general_dilated | solution.py:28
  145.3 1.3 convolution_bitcast_fusion.13
  146.7 3.1 collective-permute-start.8
  149.9 1.6 collective-permute-start.9
  151.5 2.1 convolution_bitcast_fusion.4
  153.7 1.4 convolution_bitcast_fusion.11
  155.0 1.4 convolution_bitcast_fusion.9
  156.5 1.3 convolution_bitcast_fusion.10
  157.8 1.4 convolution_bitcast_fusion.14
  159.2 1.4 convolution_bitcast_fusion.12
  160.6 1.4 convolution_bitcast_fusion.17
  162.0 1.4 convolution_bitcast_fusion.15
  163.4 1.3 convolution_bitcast_fusion.16
  175.2 132.0 %all-reduce.9.cloned.1.call-done = f32[294912]{0:T(1024)} async-done(((f32[294912]{0:T(1024)}), f32[294912]{0:T(1024)}) %all-reduce.9.cloned.1.call-update) | async-done | bytes 1179664
  307.2 1.4 dynamic-slice
  (109 shorter events, 26.4 us)
Async XLA Ops:
  7.4 61.7 %copy-start.3 = (bf16[1,64,64,128]{3,2,1,0:T(8,128)(2,1)S(1)}, bf16[1,64,64,128]{3,2,1,0:T(8,128)(2,1)}, u32[]{:S(2)}) copy-start(bf16[1,64,64,128]{3,2,1,0:T(8,128)(2,1)} %param.4) | copy-start | bytes 3145732
  7.4 61.0 %all-reduce.5.cloned.1.call-start = ((), (), s32[]{:S(2)}) async-start(), calls=%async_computation.1 | async-start | bytes 2359296 | tf_op jit(solution)/shard_map/psum | solution.py:59
  7.4 66.4 %copy-start.5 = (bf16[1,64,64,128]{3,2,1,0:T(8,128)(2,1)S(1)}, bf16[1,64,64,128]{3,2,1,0:T(8,128)(2,1)}, u32[]{:S(2)}) copy-start(bf16[1,64,64,128]{3,2,1,0:T(8,128)(2,1)} %param.5) | copy-start | bytes 3145732
  8.1 123.1 %all-reduce.7.cloned.1.call-start = ((), (), s32[]{:S(2)}) async-start(), calls=%async_computation.2 | async-start | bytes 2359296 | tf_op jit(solution)/shard_map/psum | solution.py:59
  68.4 65.7 %all-gather.2.cloned.1.call-start = ((), (), s32[]{:S(2)}) async-start(), calls=%async_computation | async-start | bytes 1216512 | tf_op jit(solution)/shard_map/all_gather | solution.py:60
  69.0 238.2 %all-reduce.9.cloned.1.call-start = ((), (), s32[]{:S(2)}) async-start(), calls=%async_computation.3 | async-start | bytes 2359296
  69.0 10.6 %collective-permute-start = (bf16[1,1,64,128]{3,2,1,0:T(8,128)(2,1)S(1)}, bf16[1,1,64,128]{3,2,1,0:T(8,128)(2,1)S(1)}, u32[]{:S(2)}, u32[]{:S(2)}) collective-permute-start(bf16[1,1,64,128]{3,2,1,0:T(8,128)(2,1)S(1)} %get-tuple-element.18), channel_id=1, source_target_pairs={{0,2},{2,4},{4,6},{1,3},{3,5},{5,7},{8,10},{10,12},{12,14},{9,11},... | collective-permute-start | bytes 49160 | tf_op jit(solution)/shard_map/ppermute | solution.py:18
  72.4 7.9 %collective-permute-start.1 = (bf16[1,1,64,128]{3,2,1,0:T(8,128)(2,1)S(1)}, bf16[1,1,64,128]{3,2,1,0:T(8,128)(2,1)S(1)}, u32[]{:S(2)}, u32[]{:S(2)}) collective-permute-start(bf16[1,1,64,128]{3,2,1,0:T(8,128)(2,1)S(1)} %get-tuple-element.17), channel_id=1, source_target_pairs={{2,0},{4,2},{6,4},{3,1},{5,3},{7,5},{10,8},{12,10},{14,12},{11,9},... | collective-permute-start | bytes 49160 | tf_op jit(solution)/shard_map/ppermute | solution.py:20
  73.8 9.3 %collective-permute-start.3 = (bf16[1,1,64,128]{3,2,1,0:T(8,128)(2,1)S(1)}, bf16[1,1,64,128]{3,2,1,0:T(8,128)(2,1)S(1)}, u32[]{:S(2)}, u32[]{:S(2)}) collective-permute-start(bf16[1,1,64,128]{3,2,1,0:T(8,128)(2,1)S(1)} %get-tuple-element.16), channel_id=1, source_target_pairs={{0,2},{2,4},{4,6},{1,3},{3,5},{5,7},{8,10},{10,12},{12,14},{9,11},... | collective-permute-start | bytes 49160 | tf_op jit(solution)/shard_map/ppermute | solution.py:18
  78.3 5.7 %collective-permute-start.4 = (bf16[1,1,64,128]{3,2,1,0:T(8,128)(2,1)S(1)}, bf16[1,1,64,128]{3,2,1,0:T(8,128)(2,1)S(1)}, u32[]{:S(2)}, u32[]{:S(2)}) collective-permute-start(bf16[1,1,64,128]{3,2,1,0:T(8,128)(2,1)S(1)} %get-tuple-element.15), channel_id=1, source_target_pairs={{2,0},{4,2},{6,4},{3,1},{5,3},{7,5},{10,8},{12,10},{14,12},{11,9},... | collective-permute-start | bytes 49160 | tf_op jit(solution)/shard_map/ppermute | solution.py:20
  80.4 3.7 %copy-start.13 = (bf16[1,1,64,128]{3,2,1,0:T(8,128)(2,1)}, bf16[1,1,64,128]{3,2,1,0:T(8,128)(2,1)S(1)}, u32[]{:S(2)}) copy-start(bf16[1,1,64,128]{3,2,1,0:T(8,128)(2,1)S(1)} %collective-permute-done.1) | copy-start | bytes 49156
  80.5 7.2 %collective-permute-start.2 = (bf16[1,66,1,128]{3,2,1,0:T(2,128)(2,1)S(1)}, bf16[1,66,1,128]{3,2,1,0:T(2,128)(2,1)S(1)}, u32[]{:S(2)}, u32[]{:S(2)}) collective-permute-start(bf16[1,66,1,128]{3,2,1,0:T(2,128)(2,1)S(1)} %get-tuple-element.13), channel_id=1, source_target_pairs={{0,1},{2,3},{4,5},{6,7},{8,9},{10,11},{12,13},{14,15},{16,17},{18,... | collective-permute-start | bytes 50696 | tf_op jit(solution)/shard_map/ppermute | solution.py:18
  81.8 5.9 %collective-permute-start.7 = (bf16[1,66,1,128]{3,2,1,0:T(2,128)(2,1)S(1)}, bf16[1,66,1,128]{3,2,1,0:T(2,128)(2,1)S(1)}, u32[]{:S(2)}, u32[]{:S(2)}) collective-permute-start(bf16[1,66,1,128]{3,2,1,0:T(2,128)(2,1)S(1)} %get-tuple-element.14), channel_id=1, source_target_pairs={{1,0},{3,2},{5,4},{7,6},{9,8},{11,10},{13,12},{15,14},{17,16},{19,... | collective-permute-start | bytes 50696 | tf_op jit(solution)/shard_map/ppermute | solution.py:20
  84.1 5.5 %collective-permute-start.5 = (bf16[1,66,1,128]{3,2,1,0:T(2,128)(2,1)S(1)}, bf16[1,66,1,128]{3,2,1,0:T(2,128)(2,1)S(1)}, u32[]{:S(2)}, u32[]{:S(2)}) collective-permute-start(bf16[1,66,1,128]{3,2,1,0:T(2,128)(2,1)S(1)} %get-tuple-element.7), channel_id=1, source_target_pairs={{0,1},{2,3},{4,5},{6,7},{8,9},{10,11},{12,13},{14,15},{16,17},{18,... | collective-permute-start | bytes 50696 | tf_op jit(solution)/shard_map/ppermute | solution.py:18
  86.4 3.2 %collective-permute-start.6 = (bf16[1,66,1,128]{3,2,1,0:T(2,128)(2,1)S(1)}, bf16[1,66,1,128]{3,2,1,0:T(2,128)(2,1)S(1)}, u32[]{:S(2)}, u32[]{:S(2)}) collective-permute-start(bf16[1,66,1,128]{3,2,1,0:T(2,128)(2,1)S(1)} %get-tuple-element.8), channel_id=1, source_target_pairs={{1,0},{3,2},{5,4},{7,6},{9,8},{11,10},{13,12},{15,14},{17,16},{19,... | collective-permute-start | bytes 50696 | tf_op jit(solution)/shard_map/ppermute | solution.py:20
  131.1 3.0 copy-start
  134.1 1.6 copy-start.15
  134.1 1.6 copy-start.9
  146.7 19.0 %collective-permute-start.8 = (bf16[1,1,64,128]{3,2,1,0:T(8,128)(2,1)S(1)}, bf16[1,1,64,128]{3,2,1,0:T(8,128)(2,1)S(1)}, u32[]{:S(2)}, u32[]{:S(2)}) collective-permute-start(bf16[1,1,64,128]{3,2,1,0:T(8,128)(2,1)S(1)} %slice.186), channel_id=1, source_target_pairs={{0,2},{2,4},{4,6},{1,3},{3,5},{5,7},{8,10},{10,12},{12,14},{9,11},... | collective-permute-start | bytes 49160 | tf_op jit(solution)/shard_map/ppermute | solution.py:18
  149.9 3.7 %copy-start.8 = (bf16[64,1,64,128]{3,0,2,1:T(8,128)(2,1)S(1)}, bf16[64,1,64,128]{3,0,2,1:T(8,128)(2,1)}, u32[]{:S(2)}) copy-start(bf16[64,1,64,128]{3,0,2,1:T(8,128)(2,1)} %copy-done.7) | copy-start | bytes 3145732
  149.9 15.8 %collective-permute-start.9 = (bf16[1,1,64,128]{3,2,1,0:T(8,128)(2,1)S(1)}, bf16[1,1,64,128]{3,2,1,0:T(8,128)(2,1)S(1)}, u32[]{:S(2)}, u32[]{:S(2)}) collective-permute-start(bf16[1,1,64,128]{3,2,1,0:T(8,128)(2,1)S(1)} %slice.189), channel_id=1, source_target_pairs={{2,0},{4,2},{6,4},{3,1},{5,3},{7,5},{10,8},{12,10},{14,12},{11,9},... | collective-permute-start | bytes 49160 | tf_op jit(solution)/shard_map/ppermute | solution.py:20
  164.8 3.6 %copy-start.6 = (bf16[1,64,64,128]{3,2,1,0:T(8,128)(2,1)S(1)}, bf16[1,64,64,128]{3,2,1,0:T(8,128)(2,1)}, u32[]{:S(2)}) copy-start(bf16[1,64,64,128]{3,2,1,0:T(8,128)(2,1)} %param.5) | copy-start | bytes 3145732
  165.8 3.6 %collective-permute-start.10 = (bf16[1,66,1,128]{3,2,1,0:T(2,128)(2,1)S(1)}, bf16[1,66,1,128]{3,2,1,0:T(2,128)(2,1)S(1)}, u32[]{:S(2)}, u32[]{:S(2)}) collective-permute-start(bf16[1,66,1,128]{3,2,1,0:T(2,128)(2,1)S(1)} %get-tuple-element.11), channel_id=1, source_target_pairs={{0,1},{2,3},{4,5},{6,7},{8,9},{10,11},{12,13},{14,15},{16,17},{18,... | collective-permute-start | bytes 50696 | tf_op jit(solution)/shard_map/ppermute | solution.py:18
  167.1 3.1 collective-permute-start.11
  (8 other events, 9.7 us)
Sparse Core Ops, SparseCore 0:
  11.3 57.0 all-reduce.4
  70.7 60.3 all-reduce.6
Sparse Core Ops, SparseCore 1:
  71.9 55.4 all-gather.1
  175.3 131.8 all-reduce.8
